TPU v7x, 32 devices: a whole 2x2x4 slice. The times are simulated.
32 devices in a mesh: blk: 8 (over z, y), grp: 4 (over x, core).
Axes of the slice: x: 2, y: 2, z: 4, core: 2. Of those that a mesh axis runs over, the one named last changes fastest.
Arguments:
- state: float32 [6, 131072], P(None, ('blk', 'grp')), may hold values from -6 to 6
- mass: float32 [131072], P(('blk', 'grp')), may hold values from 1.5258789e-06 to 3.8146973e-05
- active_index: int32 [8, 32], P('blk'), may hold values from 0 to 16383, as said below
- counts: int32 [8], P('blk'), may hold values from 8 to 32, as said below
Outputs:
- acc_jerk: float32 [6, 256], P(None, 'blk')
- potential: float32 [256], P('blk')
Inputs may be any that keep to these rules, and one draw needn't show every extreme that they name: `active_index`: each row holds 32 different star numbers of its slot block; only the first counts[b] entries of row b are active. `counts`: in every draw some slot is full, with 32 active stars.
All inputs are finite; a program needn't handle non-finite values.
Results may differ from a plain program's by a relative error of at most 0.0003.
Values sent between devices are 32-bit elements; how exact they have to be, the bound alone decides.
A program may use at most 64 MiB of HBM per device.

v0:
```python
import jax
import jax.numpy as jnp
from jax import lax
from jax.sharding import PartitionSpec as P

softening = 0.001


def shifted(block, axis, distance):
    devices = range(lax.axis_size(axis))
    route = [((i - distance) % len(devices), i) for i in devices]
    return lax.ppermute(block, axis, route)


def pair_terms(active, field):
    dpos = field[0:3, None, :] - active[0:3, :, None]
    dvel = field[3:6, None, :] - active[3:6, :, None]
    raw = jnp.sum(dpos * dpos, axis=0)
    weight = jnp.where(raw == 0.0, 0.0, field[6][None, :])
    inv = lax.rsqrt(raw + softening)
    first = weight * inv
    third = first * inv * inv
    along = jnp.sum(dpos * dvel, axis=0)
    fifth = 3.0 * along * third * inv * inv
    accel = jnp.sum(third[None] * dpos, axis=-1)
    jerk = jnp.sum(third[None] * dvel - fifth[None] * dpos, axis=-1)
    pot = -jnp.sum(first, axis=-1)
    return jnp.concatenate([accel, jerk, pot[None]], axis=0)


def live_terms(active, field):
    return pair_terms(active, field)


def on_device(state, mass, active_index, counts):
    blocks = lax.axis_size("blk")
    capacity = active_index.shape[1]
    picks = active_index[0]
    count_live = counts[0]
    slot_state = lax.all_gather(state, "grp", axis=1, tiled=True)
    active = jnp.take(slot_state, picks, axis=1)
    field = jnp.concatenate([state, mass[None, :]], axis=0)

    def turn_one(step, carry):
        summed, moving = carry
        moving = shifted(moving, "blk", 1)
        return (summed + live_terms(active, moving), moving)

    start = live_terms(active, field)
    total = lax.fori_loop(1, blocks, turn_one, (start, field))[0]
    live = jnp.arange(capacity, dtype=jnp.int32) < count_live
    total = jnp.where(live[None, :], total, 0.0)
    summed = lax.psum(total, "grp")
    return (summed[0:6], summed[6])


def solution(mesh):
    placed = (P(None, ("blk", "grp")), P(("blk", "grp")), P("blk", None), P("blk"))
    return jax.shard_map(
        on_device, mesh=mesh, in_specs=placed, out_specs=(P(None, "blk"), P("blk")), check_vma=False
    )
```

profile of v0, /device:TPU:0, one launch (start us, length us, event | category | flops | bytes accessed | tf_op | source)
XLA Modules:
  0.0 132.4 jit_solution(1626110730015682410)
XLA Ops:
  0.6 1.5 %copy.10 = f32[6,4096]{0,1:T(8,128)S(1)} copy(f32[6,4096]{1,0:T(8,128)} %param.6) | data formatting | bytes 196608 | tf_op args[0]
  2.2 52.0 %all_gather.3 = f32[6,16384]{0,1:T(8,128)} all-gather(f32[6,4096]{0,1:T(8,128)S(1)} %copy.10), channel_id=1, replica_groups=mesh['blk'=8,'grp'=4] {'grp'}, dimensions={1}, use_global_device_ids=true | all-gather | bytes 491520 | tf_op jit(solution)/shard_map/all_gather | solution.py:40
  54.3 4.0 %gather_fusion = f32[32,6]{1,0:T(8,128)S(1)} fusion(f32[6,16384]{0,1:T(8,128)} %all_gather.3, s32[1024]{0:T(1024)S(1)} %pad_clamp_fusion), kind=kCustom, calls=%fused_computation | custom fusion | bytes 1664 | tf_op jit(solution)/shard_map/jit(_take)/gather | solution.py:41
  58.6 0.4 fusion.10
  59.0 0.3 multiply_multiply_fusion.2
  59.3 0.6 fusion.9
  60.1 65.4 %while.12 = (s32[]{:T(128)}, f32[7,32]{1,0:T(8,128)S(1)}, f32[7,4096]{1,0:T(8,128)S(1)}, f32[6,32]{1,0:T(8,128)S(1)}, s32[]{:T(128)}) while((s32[]{:T(128)}, f32[7,32]{1,0:T(8,128)S(1)}, f32[7,4096]{1,0:T(8,128)S(1)}, f32[6,32]{1,0:T(8,128)S(1)}, s32[]{:T(128)}) %tuple.46), condition=%wide.region_11.12_spmd, body=%wide.region_5.11_spmd.sunk | while | flops 6685154 | bytes 5331813 | solution.py:50
  60.1 1.6 %collective-permute-start = (f32[7,4096]{1,0:T(8,128)S(1)}, f32[7,4096]{1,0:T(8,128)S(1)}, u32[]{:S(2)}, u32[]{:S(2)}) collective-permute-start(f32[7,4096]{1,0:T(8,128)S(1)} %get-tuple-element.117), channel_id=1, source_target_pairs={{28,0},{0,4},{4,8},{8,12},{12,16},{16,20},{20,24},{24,28},{29,1},{... | collective-permute-start | bytes 344072 | tf_op jit(solution)/shard_map/while/body/eval_jaxpr/ppermute | solution.py:12
  61.7 7.1 %collective-permute-done = f32[7,4096]{1,0:T(8,128)S(1)} collective-permute-done((f32[7,4096]{1,0:T(8,128)S(1)}, f32[7,4096]{1,0:T(8,128)S(1)}, u32[]{:S(2)}, u32[]{:S(2)}) %collective-permute-start) | collective-permute-done | bytes 114720 | tf_op jit(solution)/shard_map/while/body/eval_jaxpr/ppermute | solution.py:12
  68.8 0.4 fusion.23
  69.2 0.3 multiply_multiply_fusion.5
  69.5 0.6 fusion.24
  70.3 7.7 %collective-permute-done = f32[7,4096]{1,0:T(8,128)S(1)} collective-permute-done((f32[7,4096]{1,0:T(8,128)S(1)}, f32[7,4096]{1,0:T(8,128)S(1)}, u32[]{:S(2)}, u32[]{:S(2)}) %collective-permute-start) | collective-permute-done | bytes 114720 | tf_op jit(solution)/shard_map/while/body/eval_jaxpr/ppermute | solution.py:12
  78.0 0.4 fusion.23
  78.8 0.6 fusion.24
  79.6 7.6 %collective-permute-done = f32[7,4096]{1,0:T(8,128)S(1)} collective-permute-done((f32[7,4096]{1,0:T(8,128)S(1)}, f32[7,4096]{1,0:T(8,128)S(1)}, u32[]{:S(2)}, u32[]{:S(2)}) %collective-permute-start) | collective-permute-done | bytes 114720 | tf_op jit(solution)/shard_map/while/body/eval_jaxpr/ppermute | solution.py:12
  87.2 0.4 fusion.23
  88.0 0.6 fusion.24
  88.8 7.6 %collective-permute-done = f32[7,4096]{1,0:T(8,128)S(1)} collective-permute-done((f32[7,4096]{1,0:T(8,128)S(1)}, f32[7,4096]{1,0:T(8,128)S(1)}, u32[]{:S(2)}, u32[]{:S(2)}) %collective-permute-start) | collective-permute-done | bytes 114720 | tf_op jit(solution)/shard_map/while/body/eval_jaxpr/ppermute | solution.py:12
  96.4 0.4 fusion.23
  97.2 0.6 fusion.24
  97.9 7.6 %collective-permute-done = f32[7,4096]{1,0:T(8,128)S(1)} collective-permute-done((f32[7,4096]{1,0:T(8,128)S(1)}, f32[7,4096]{1,0:T(8,128)S(1)}, u32[]{:S(2)}, u32[]{:S(2)}) %collective-permute-start) | collective-permute-done | bytes 114720 | tf_op jit(solution)/shard_map/while/body/eval_jaxpr/ppermute | solution.py:12
  105.6 0.4 fusion.23
  106.4 0.6 fusion.24
  107.1 7.6 %collective-permute-done = f32[7,4096]{1,0:T(8,128)S(1)} collective-permute-done((f32[7,4096]{1,0:T(8,128)S(1)}, f32[7,4096]{1,0:T(8,128)S(1)}, u32[]{:S(2)}, u32[]{:S(2)}) %collective-permute-start) | collective-permute-done | bytes 114720 | tf_op jit(solution)/shard_map/while/body/eval_jaxpr/ppermute | solution.py:12
  114.8 0.4 fusion.23
  115.6 0.6 fusion.24
  116.3 7.6 %collective-permute-done = f32[7,4096]{1,0:T(8,128)S(1)} collective-permute-done((f32[7,4096]{1,0:T(8,128)S(1)}, f32[7,4096]{1,0:T(8,128)S(1)}, u32[]{:S(2)}, u32[]{:S(2)}) %collective-permute-start) | collective-permute-done | bytes 114720 | tf_op jit(solution)/shard_map/while/body/eval_jaxpr/ppermute | solution.py:12
  124.0 0.4 fusion.23
  124.8 0.6 fusion.24
  126.1 5.7 %psum.7 = f32[7,32]{1,0:T(8,128)S(1)} all-reduce(f32[7,32]{1,0:T(8,128)S(1)} %broadcast_select_fusion), channel_id=1, replica_groups=mesh['blk'=8,'grp'=4] {'grp'}, use_global_device_ids=true, to_apply=%region_12.13 | all-reduce | flops 224 | bytes 1792 | tf_op jit(solution)/shard_map/psum | solution.py:53
  131.8 0.5 slice_bitcast_fusion
  (76 shorter events, 3.4 us)
Async XLA Ops:
  2.2 52.1 %copy-start.3 = (s32[1,32]{1,0:T(1,128)S(1)}, s32[1,32]{1,0:T(1,128)}, u32[]{:S(2)}) copy-start(s32[1,32]{1,0:T(1,128)} %param.8) | copy-start | bytes 388
  2.2 56.3 %copy-start = (f32[6,4096]{1,0:T(8,128)S(1)}, f32[6,4096]{1,0:T(8,128)}, u32[]{:S(2)}) copy-start(f32[6,4096]{1,0:T(8,128)} %param.6) | copy-start | bytes 294916
  54.2 4.8 %copy-start.1 = (f32[4096]{0:T(1024)S(1)}, f32[4096]{0:T(1024)}, u32[]{:S(2)}) copy-start(f32[4096]{0:T(1024)} %param.7) | copy-start | bytes 49156
  60.1 8.6 %collective-permute-start = (f32[7,4096]{1,0:T(8,128)S(1)}, f32[7,4096]{1,0:T(8,128)S(1)}, u32[]{:S(2)}, u32[]{:S(2)}) collective-permute-start(f32[7,4096]{1,0:T(8,128)S(1)} %get-tuple-element.117), channel_id=1, source_target_pairs={{28,0},{0,4},{4,8},{8,12},{12,16},{16,20},{20,24},{24,28},{29,1},{... | collective-permute-start | bytes 344072 | tf_op jit(solution)/shard_map/while/body/eval_jaxpr/ppermute | solution.py:12
  70.2 7.8 %collective-permute-start = (f32[7,4096]{1,0:T(8,128)S(1)}, f32[7,4096]{1,0:T(8,128)S(1)}, u32[]{:S(2)}, u32[]{:S(2)}) collective-permute-start(f32[7,4096]{1,0:T(8,128)S(1)} %get-tuple-element.117), channel_id=1, source_target_pairs={{28,0},{0,4},{4,8},{8,12},{12,16},{16,20},{20,24},{24,28},{29,1},{... | collective-permute-start | bytes 344072 | tf_op jit(solution)/shard_map/while/body/eval_jaxpr/ppermute | solution.py:12
  79.5 7.7 %collective-permute-start = (f32[7,4096]{1,0:T(8,128)S(1)}, f32[7,4096]{1,0:T(8,128)S(1)}, u32[]{:S(2)}, u32[]{:S(2)}) collective-permute-start(f32[7,4096]{1,0:T(8,128)S(1)} %get-tuple-element.117), channel_id=1, source_target_pairs={{28,0},{0,4},{4,8},{8,12},{12,16},{16,20},{20,24},{24,28},{29,1},{... | collective-permute-start | bytes 344072 | tf_op jit(solution)/shard_map/while/body/eval_jaxpr/ppermute | solution.py:12
  88.7 7.7 %collective-permute-start = (f32[7,4096]{1,0:T(8,128)S(1)}, f32[7,4096]{1,0:T(8,128)S(1)}, u32[]{:S(2)}, u32[]{:S(2)}) collective-permute-start(f32[7,4096]{1,0:T(8,128)S(1)} %get-tuple-element.117), channel_id=1, source_target_pairs={{28,0},{0,4},{4,8},{8,12},{12,16},{16,20},{20,24},{24,28},{29,1},{... | collective-permute-start | bytes 344072 | tf_op jit(solution)/shard_map/while/body/eval_jaxpr/ppermute | solution.py:12
  97.9 7.7 %collective-permute-start = (f32[7,4096]{1,0:T(8,128)S(1)}, f32[7,4096]{1,0:T(8,128)S(1)}, u32[]{:S(2)}, u32[]{:S(2)}) collective-permute-start(f32[7,4096]{1,0:T(8,128)S(1)} %get-tuple-element.117), channel_id=1, source_target_pairs={{28,0},{0,4},{4,8},{8,12},{12,16},{16,20},{20,24},{24,28},{29,1},{... | collective-permute-start | bytes 344072 | tf_op jit(solution)/shard_map/while/body/eval_jaxpr/ppermute | solution.py:12
  107.1 7.7 %collective-permute-start = (f32[7,4096]{1,0:T(8,128)S(1)}, f32[7,4096]{1,0:T(8,128)S(1)}, u32[]{:S(2)}, u32[]{:S(2)}) collective-permute-start(f32[7,4096]{1,0:T(8,128)S(1)} %get-tuple-element.117), channel_id=1, source_target_pairs={{28,0},{0,4},{4,8},{8,12},{12,16},{16,20},{20,24},{24,28},{29,1},{... | collective-permute-start | bytes 344072 | tf_op jit(solution)/shard_map/while/body/eval_jaxpr/ppermute | solution.py:12
  116.3 7.7 %collective-permute-start = (f32[7,4096]{1,0:T(8,128)S(1)}, f32[7,4096]{1,0:T(8,128)S(1)}, u32[]{:S(2)}, u32[]{:S(2)}) collective-permute-start(f32[7,4096]{1,0:T(8,128)S(1)} %get-tuple-element.117), channel_id=1, source_target_pairs={{28,0},{0,4},{4,8},{8,12},{12,16},{16,20},{20,24},{24,28},{29,1},{... | collective-permute-start | bytes 344072 | tf_op jit(solution)/shard_map/while/body/eval_jaxpr/ppermute | solution.py:12
  131.8 0.6 copy-start.2
where the time goes:
time: 133 us; the launch traced here: 132 us
  blocking collectives  57.7 us (43%)
  waiting for transfers between devices  53 us (40%)
  other arithmetic  11.1 us (8%)
  local copies, waits for them, and re-layouts  6.87 us (5%)
  starting transfers between devices  1.92 us (1%)
  between operations  1.38 us (1%)
    ppermute x7, waiting for transfers between devices, shifted(): return lax.ppermute(block, axis, route)  53 us
    all_gather x1, blocking collectives, on_device(): slot_state = lax.all_gather(state, 'grp', axis=1, tiled=True)  52 us
    psum x1, blocking collectives, on_device(): summed = lax.psum(total, 'grp')  5.67 us
    reduce_sum x8, other arithmetic, pair_terms(): accel = jnp.sum(third[None] * dpos, axis=-1)  5.02 us
    gather x1, local copies, waits for them, and re-layouts, on_device(): active = jnp.take(slot_state, picks, axis=1)  3.95 us
    reduce_sum x8, other arithmetic, pair_terms(): along = jnp.sum(dpos * dvel, axis=0)  3.27 us
  transfers between devices with their start and end apart: 7, of which 7 were waited for; matrix products, arithmetic and copies ran while one was open for 0% of the time, Pallas kernels for 0%

commit v1 on v0

--- a/solution.py
+++ b/solution.py
@@ -37,7 +37,16 @@
     capacity = active_index.shape[1]
     picks = active_index[0]
     count_live = counts[0]
-    slot_state = lax.all_gather(state, "grp", axis=1, tiled=True)
+    unite_surface = lambda incoming_x: jnp.concatenate(
+        jax.lax.all_to_all(
+            jnp.stack(jax.lax.axis_size("grp") * [incoming_x]),
+            axis_name="grp",
+            split_axis=0,
+            concat_axis=0,
+        ),
+        axis=1,
+    )
+    slot_state = unite_surface(state)
     active = jnp.take(slot_state, picks, axis=1)
     field = jnp.concatenate([state, mass[None, :]], axis=0)
 

time: 133 us -> 97.8 us (0.74)
  blocking collectives: 57.7 us -> 5.67 us
  waiting for transfers between devices: 53 us -> 60.1 us
  local copies, waits for them, and re-layouts: 6.87 us -> 12 us
  starting transfers between devices: 1.92 us -> 6.84 us
    all_gather x1 -> x0, blocking collectives: 52 us -> none  [on_device(): slot_state = lax.all_gather(state, 'grp', axis=1, tiled=True)]
    all_to_all x0 -> x1, waiting for transfers between devices: none -> 8.02 us  [on_device(): jax.lax.all_to_all(jnp.stack(jax.lax.axis_size('grp') * [incoming_x]), ax...]
    reshape x0 -> x1, local copies, waits for them, and re-layouts: none -> 4.87 us  [on_device(): jnp.concatenate(jax.lax.all_to_all(jnp.stack(jax.lax.axis_size('grp') * [...]
    all_to_all x0 -> x1, starting transfers between devices: none -> 4.24 us  [on_device(): jax.lax.all_to_all(jnp.stack(jax.lax.axis_size('grp') * [incoming_x]), ax...]
    another operation x0 -> x1, local copies, waits for them, and re-layouts: none -> 1.79 us  [on_device(): jnp.stack(jax.lax.axis_size('grp') * [incoming_x])]
    unnamed x9 -> x8, local copies, waits for them, and re-layouts: 1.63 us -> 0.09 us
  transfers between devices with their start and end apart: 7 -> 8, of which waited for: 7 -> 8; matrix products, arithmetic and copies ran while one was open for 0% -> 0% of each run, Pallas kernels for 0% -> 0%
where the time goes in v1:
time: 97.8 us; the launch traced here: 97.5 us
  waiting for transfers between devices  60.1 us (61%)
  local copies, waits for them, and re-layouts  12 us (12%)
  other arithmetic  11.1 us (11%)
  starting transfers between devices  6.84 us (7%)
  blocking collectives  5.67 us (6%)
  between operations  1.39 us (1%)
    ppermute x7, waiting for transfers between devices, shifted(): return lax.ppermute(block, axis, route)  52.1 us
    all_to_all x1, waiting for transfers between devices, on_device(): jax.lax.all_to_all(jnp.stack(jax.lax.axis_size('grp') * [incoming_x]), ax...  8.02 us
    psum x1, blocking collectives, on_device(): summed = lax.psum(total, 'grp')  5.67 us
    reduce_sum x8, other arithmetic, pair_terms(): accel = jnp.sum(third[None] * dpos, axis=-1)  5.02 us
    reshape x1, local copies, waits for them, and re-layouts, on_device(): jnp.concatenate(jax.lax.all_to_all(jnp.stack(jax.lax.axis_size('grp') * [...  4.87 us
    all_to_all x1, starting transfers between devices, on_device(): jax.lax.all_to_all(jnp.stack(jax.lax.axis_size('grp') * [incoming_x]), ax...  4.24 us
    gather x1, local copies, waits for them, and re-layouts, on_device(): active = jnp.take(slot_state, picks, axis=1)  3.95 us
    reduce_sum x8, other arithmetic, pair_terms(): along = jnp.sum(dpos * dvel, axis=0)  3.29 us
  transfers between devices with their start and end apart: 8, of which 8 were waited for; matrix products, arithmetic and copies ran while one was open for 0% of the time, Pallas kernels for 0%

profile of v1, /device:TPU:0, one launch (start us, length us, event | category | flops | bytes accessed | tf_op | source)
XLA Modules:
  0.0 97.5 jit_solution(11140325787586992840)
XLA Ops:
  0.7 1.8 %stack.2 = f32[4,6,4096]{2,1,0:T(8,128)} broadcast(f32[6,4096]{1,0:T(8,128)} %param.6), dimensions={1,2} | broadcast | bytes 491520 | tf_op jit(solution)/shard_map/stack | solution.py:42
  2.5 4.2 %all-to-all-start = ((f32[4,6,4096]{2,1,0:T(8,128)}), f32[4,6,4096]{2,1,0:T(8,128)S(1)}, u32[]{:S(2)}, u32[]{:S(2)}) async-start(f32[4,6,4096]{2,1,0:T(8,128)} %stack.2), calls=%async_computation | async-start | bytes 1048576 | tf_op jit(solution)/shard_map/all_to_all | solution.py:41
  7.5 8.0 %all-to-all-done = f32[4,6,4096]{2,1,0:T(8,128)S(1)} async-done(((f32[4,6,4096]{2,1,0:T(8,128)}), f32[4,6,4096]{2,1,0:T(8,128)S(1)}, u32[]{:S(2)}, u32[]{:S(2)}) %all-to-all-start) | async-done | bytes 393248 | tf_op jit(solution)/shard_map/all_to_all | solution.py:41
  15.5 4.9 %copy.14 = f32[6,4,4096]{0,2,1:T(8,128)} copy(f32[6,4,4096]{2,0,1:T(8,128)S(1)} %bitcast.26) | data formatting | bytes 786432 | tf_op jit(solution)/shard_map/reshape | solution.py:40
  20.4 4.0 %gather_fusion = f32[32,6]{1,0:T(8,128)S(1)} fusion(f32[6,16384]{0,1:T(8,128)} %bitcast.25, s32[1024]{0:T(1024)S(1)} %pad_clamp_fusion), kind=kCustom, calls=%fused_computation | custom fusion | bytes 1664 | tf_op jit(solution)/shard_map/jit(_take)/gather | solution.py:50
  24.7 0.4 fusion.10
  25.5 0.6 fusion.9
  26.1 65.1 %while.12 = (s32[]{:T(128)}, f32[7,32]{1,0:T(8,128)S(1)}, f32[7,4096]{1,0:T(8,128)S(1)}, f32[6,32]{1,0:T(8,128)S(1)}, s32[]{:T(128)}) while((s32[]{:T(128)}, f32[7,32]{1,0:T(8,128)S(1)}, f32[7,4096]{1,0:T(8,128)S(1)}, f32[6,32]{1,0:T(8,128)S(1)}, s32[]{:T(128)}) %tuple.47), condition=%wide.region_11.12_spmd, body=%wide.region_5.11_spmd.sunk | while | flops 6685154 | bytes 5331813 | solution.py:59
  26.1 2.3 %collective-permute-start = (f32[7,4096]{1,0:T(8,128)S(1)}, f32[7,4096]{1,0:T(8,128)S(1)}, u32[]{:S(2)}, u32[]{:S(2)}) collective-permute-start(f32[7,4096]{1,0:T(8,128)S(1)} %get-tuple-element.121), channel_id=1, source_target_pairs={{28,0},{0,4},{4,8},{8,12},{12,16},{16,20},{20,24},{24,28},{29,1},{... | collective-permute-start | bytes 344072 | tf_op jit(solution)/shard_map/while/body/eval_jaxpr/ppermute | solution.py:12
  28.4 6.2 %collective-permute-done = f32[7,4096]{1,0:T(8,128)S(1)} collective-permute-done((f32[7,4096]{1,0:T(8,128)S(1)}, f32[7,4096]{1,0:T(8,128)S(1)}, u32[]{:S(2)}, u32[]{:S(2)}) %collective-permute-start) | collective-permute-done | bytes 114720 | tf_op jit(solution)/shard_map/while/body/eval_jaxpr/ppermute | solution.py:12
  34.6 0.4 fusion.23
  35.4 0.6 fusion.24
  36.2 7.6 %collective-permute-done = f32[7,4096]{1,0:T(8,128)S(1)} collective-permute-done((f32[7,4096]{1,0:T(8,128)S(1)}, f32[7,4096]{1,0:T(8,128)S(1)}, u32[]{:S(2)}, u32[]{:S(2)}) %collective-permute-start) | collective-permute-done | bytes 114720 | tf_op jit(solution)/shard_map/while/body/eval_jaxpr/ppermute | solution.py:12
  43.8 0.4 fusion.23
  44.6 0.6 fusion.24
  45.4 7.6 %collective-permute-done = f32[7,4096]{1,0:T(8,128)S(1)} collective-permute-done((f32[7,4096]{1,0:T(8,128)S(1)}, f32[7,4096]{1,0:T(8,128)S(1)}, u32[]{:S(2)}, u32[]{:S(2)}) %collective-permute-start) | collective-permute-done | bytes 114720 | tf_op jit(solution)/shard_map/while/body/eval_jaxpr/ppermute | solution.py:12
  53.0 0.4 fusion.23
  53.8 0.6 fusion.24
  54.6 7.6 %collective-permute-done = f32[7,4096]{1,0:T(8,128)S(1)} collective-permute-done((f32[7,4096]{1,0:T(8,128)S(1)}, f32[7,4096]{1,0:T(8,128)S(1)}, u32[]{:S(2)}, u32[]{:S(2)}) %collective-permute-start) | collective-permute-done | bytes 114720 | tf_op jit(solution)/shard_map/while/body/eval_jaxpr/ppermute | solution.py:12
  62.2 0.4 fusion.23
  63.0 0.6 fusion.24
  63.7 7.6 %collective-permute-done = f32[7,4096]{1,0:T(8,128)S(1)} collective-permute-done((f32[7,4096]{1,0:T(8,128)S(1)}, f32[7,4096]{1,0:T(8,128)S(1)}, u32[]{:S(2)}, u32[]{:S(2)}) %collective-permute-start) | collective-permute-done | bytes 114720 | tf_op jit(solution)/shard_map/while/body/eval_jaxpr/ppermute | solution.py:12
  71.4 0.4 fusion.23
  72.2 0.6 fusion.24
  72.9 7.6 %collective-permute-done = f32[7,4096]{1,0:T(8,128)S(1)} collective-permute-done((f32[7,4096]{1,0:T(8,128)S(1)}, f32[7,4096]{1,0:T(8,128)S(1)}, u32[]{:S(2)}, u32[]{:S(2)}) %collective-permute-start) | collective-permute-done | bytes 114720 | tf_op jit(solution)/shard_map/while/body/eval_jaxpr/ppermute | solution.py:12
  80.6 0.4 fusion.23
  81.4 0.6 fusion.24
  82.1 7.6 %collective-permute-done = f32[7,4096]{1,0:T(8,128)S(1)} collective-permute-done((f32[7,4096]{1,0:T(8,128)S(1)}, f32[7,4096]{1,0:T(8,128)S(1)}, u32[]{:S(2)}, u32[]{:S(2)}) %collective-permute-start) | collective-permute-done | bytes 114720 | tf_op jit(solution)/shard_map/while/body/eval_jaxpr/ppermute | solution.py:12
  89.8 0.4 fusion.23
  90.6 0.6 fusion.24
  91.3 5.7 %psum.7 = f32[7,32]{1,0:T(8,128)S(1)} all-reduce(f32[7,32]{1,0:T(8,128)S(1)} %broadcast_select_fusion), channel_id=1, replica_groups=mesh['blk'=8,'grp'=4] {'grp'}, use_global_device_ids=true, to_apply=%region_12.13 | all-reduce | flops 224 | bytes 1792 | tf_op jit(solution)/shard_map/psum | solution.py:62
  96.9 0.5 slice_bitcast_fusion
  (78 shorter events, 4.0 us)
Async XLA Ops:
  0.6 6.1 %copy-start = (f32[6,4096]{1,0:T(8,128)S(1)}, f32[6,4096]{1,0:T(8,128)}, u32[]{:S(2)}) copy-start(f32[6,4096]{1,0:T(8,128)} %param.6) | copy-start | bytes 294916
  0.6 6.1 %copy-start.3 = (s32[1,32]{1,0:T(1,128)S(1)}, s32[1,32]{1,0:T(1,128)}, u32[]{:S(2)}) copy-start(s32[1,32]{1,0:T(1,128)} %param.8) | copy-start | bytes 388
  0.6 6.1 %copy-start.1 = (f32[4096]{0:T(1024)S(1)}, f32[4096]{0:T(1024)}, u32[]{:S(2)}) copy-start(f32[4096]{0:T(1024)} %param.7) | copy-start | bytes 49156
  2.5 13.1 %all-to-all-start = ((f32[4,6,4096]{2,1,0:T(8,128)}), f32[4,6,4096]{2,1,0:T(8,128)S(1)}, u32[]{:S(2)}, u32[]{:S(2)}) async-start(f32[4,6,4096]{2,1,0:T(8,128)} %stack.2), calls=%async_computation | async-start | bytes 1048576 | tf_op jit(solution)/shard_map/all_to_all | solution.py:41
  26.1 8.5 %collective-permute-start = (f32[7,4096]{1,0:T(8,128)S(1)}, f32[7,4096]{1,0:T(8,128)S(1)}, u32[]{:S(2)}, u32[]{:S(2)}) collective-permute-start(f32[7,4096]{1,0:T(8,128)S(1)} %get-tuple-element.121), channel_id=1, source_target_pairs={{28,0},{0,4},{4,8},{8,12},{12,16},{16,20},{20,24},{24,28},{29,1},{... | collective-permute-start | bytes 344072 | tf_op jit(solution)/shard_map/while/body/eval_jaxpr/ppermute | solution.py:12
  36.1 7.7 %collective-permute-start = (f32[7,4096]{1,0:T(8,128)S(1)}, f32[7,4096]{1,0:T(8,128)S(1)}, u32[]{:S(2)}, u32[]{:S(2)}) collective-permute-start(f32[7,4096]{1,0:T(8,128)S(1)} %get-tuple-element.121), channel_id=1, source_target_pairs={{28,0},{0,4},{4,8},{8,12},{12,16},{16,20},{20,24},{24,28},{29,1},{... | collective-permute-start | bytes 344072 | tf_op jit(solution)/shard_map/while/body/eval_jaxpr/ppermute | solution.py:12
  45.3 7.7 %collective-permute-start = (f32[7,4096]{1,0:T(8,128)S(1)}, f32[7,4096]{1,0:T(8,128)S(1)}, u32[]{:S(2)}, u32[]{:S(2)}) collective-permute-start(f32[7,4096]{1,0:T(8,128)S(1)} %get-tuple-element.121), channel_id=1, source_target_pairs={{28,0},{0,4},{4,8},{8,12},{12,16},{16,20},{20,24},{24,28},{29,1},{... | collective-permute-start | bytes 344072 | tf_op jit(solution)/shard_map/while/body/eval_jaxpr/ppermute | solution.py:12
  54.5 7.7 %collective-permute-start = (f32[7,4096]{1,0:T(8,128)S(1)}, f32[7,4096]{1,0:T(8,128)S(1)}, u32[]{:S(2)}, u32[]{:S(2)}) collective-permute-start(f32[7,4096]{1,0:T(8,128)S(1)} %get-tuple-element.121), channel_id=1, source_target_pairs={{28,0},{0,4},{4,8},{8,12},{12,16},{16,20},{20,24},{24,28},{29,1},{... | collective-permute-start | bytes 344072 | tf_op jit(solution)/shard_map/while/body/eval_jaxpr/ppermute | solution.py:12
  63.7 7.7 %collective-permute-start = (f32[7,4096]{1,0:T(8,128)S(1)}, f32[7,4096]{1,0:T(8,128)S(1)}, u32[]{:S(2)}, u32[]{:S(2)}) collective-permute-start(f32[7,4096]{1,0:T(8,128)S(1)} %get-tuple-element.121), channel_id=1, source_target_pairs={{28,0},{0,4},{4,8},{8,12},{12,16},{16,20},{20,24},{24,28},{29,1},{... | collective-permute-start | bytes 344072 | tf_op jit(solution)/shard_map/while/body/eval_jaxpr/ppermute | solution.py:12
  72.9 7.7 %collective-permute-start = (f32[7,4096]{1,0:T(8,128)S(1)}, f32[7,4096]{1,0:T(8,128)S(1)}, u32[]{:S(2)}, u32[]{:S(2)}) collective-permute-start(f32[7,4096]{1,0:T(8,128)S(1)} %get-tuple-element.121), channel_id=1, source_target_pairs={{28,0},{0,4},{4,8},{8,12},{12,16},{16,20},{20,24},{24,28},{29,1},{... | collective-permute-start | bytes 344072 | tf_op jit(solution)/shard_map/while/body/eval_jaxpr/ppermute | solution.py:12
  82.1 7.7 %collective-permute-start = (f32[7,4096]{1,0:T(8,128)S(1)}, f32[7,4096]{1,0:T(8,128)S(1)}, u32[]{:S(2)}, u32[]{:S(2)}) collective-permute-start(f32[7,4096]{1,0:T(8,128)S(1)} %get-tuple-element.121), channel_id=1, source_target_pairs={{28,0},{0,4},{4,8},{8,12},{12,16},{16,20},{20,24},{24,28},{29,1},{... | collective-permute-start | bytes 344072 | tf_op jit(solution)/shard_map/while/body/eval_jaxpr/ppermute | solution.py:12
  96.9 0.6 copy-start.2
